TPU v7x, 128 devices: a whole 4x4x4 slice. The times are simulated.
128 devices in a mesh: lat: 8 (over y, z_lo), lon: 16 (over z_hi, x, core).
Axes of the slice: x: 4, y: 4, z: 4 (z_hi: 2, z_lo: 2; z = z_hi * 2 + z_lo), core: 2. Of those that a mesh axis runs over, the one named last changes fastest.
Arguments:
- state: bfloat16 [1024, 2048, 128], P('lat', 'lon'), may hold values from -6 to 6
- edge_metric: float32 [9, 1024, 2048], P(None, 'lat', 'lon'), may hold values from 0.1 to 1
- stencil_coef: float32 [2, 9, 128], replicated, may hold values from -4 to 4
- norm_gain: float32 [2, 128], replicated, may hold values from 0.25 to 1.75
- biases: float32 [2, 4, 128], replicated, may hold values from -3 to 3
- weights: bfloat16 [2, 896, 128], P(None, ('lat', 'lon')), may hold values from -0.5 to 0.5
Outputs:
- refined: bfloat16 [1024, 2048, 128], P('lat', 'lon')
All inputs are finite; a program needn't handle non-finite values.
Results may differ from a plain program's by a relative error of at most 0.0069.
Values may be sent and summed in bfloat16 or wider, within the bound.
A program may use at most 128 MiB of HBM per device.

v0:
```python
import jax
import jax.numpy as jnp
from jax import lax
from jax.sharding import PartitionSpec as P

KMAT = 7
ITERS = 2
EPSILON = 1e-05


def extended(cells, sides, width, closed):
    for axis, dim in sides:
        count = lax.axis_size(axis)
        ends = count if closed else count - 1
        head = lax.slice_in_dim(cells, 0, width, axis=dim)
        tail = lax.slice_in_dim(cells, cells.shape[dim] - width, cells.shape[dim], axis=dim)
        cells = jnp.concatenate(
            [
                lax.ppermute(tail, axis, [(i, (i + 1) % count) for i in range(ends)]),
                cells,
                lax.ppermute(head, axis, [((i + 1) % count, i) for i in range(ends)]),
            ],
            axis=dim,
        )
    return cells


def passed_along(block, axis, distance):
    devices = range(lax.axis_size(axis))
    route = [((i - distance) % len(devices), i) for i in devices]
    return lax.ppermute(block, axis, route)


def grid_update(padded_rows, metric_rows, state_rows, coef, gain, bias, mats):
    row_count = state_rows.shape[0]
    col_count = state_rows.shape[1]
    channels = state_rows.shape[2]
    summed = jnp.zeros(state_rows.shape, jnp.float32)
    for lat_step in range(3):
        for lon_step in range(3):
            direction = 3 * lat_step + lon_step
            view = padded_rows[
                lat_step : lat_step + row_count, lon_step : lon_step + col_count
            ].astype(jnp.float32)
            summed = summed + metric_rows[direction][:, :, None] * coef[direction] * view
    scale = lax.rsqrt(jnp.mean(summed * summed, axis=-1, keepdims=True) + EPSILON)
    normed = (summed * scale * gain).astype(jnp.bfloat16).reshape(-1, channels)
    hidden = state_rows.reshape(-1, channels)
    message = (jnp.dot(normed, mats[0], preferred_element_type=jnp.float32) + bias[0]).astype(
        jnp.bfloat16
    )
    update = jax.nn.sigmoid(
        jnp.dot(message, mats[1], preferred_element_type=jnp.float32)
        + jnp.dot(hidden, mats[4], preferred_element_type=jnp.float32)
        + bias[1]
    )
    reset = jax.nn.sigmoid(
        jnp.dot(message, mats[2], preferred_element_type=jnp.float32)
        + jnp.dot(hidden, mats[5], preferred_element_type=jnp.float32)
        + bias[2]
    )
    candidate = jnp.tanh(
        jnp.dot(message, mats[3], preferred_element_type=jnp.float32)
        + bias[3]
        + reset * jnp.dot(hidden, mats[6], preferred_element_type=jnp.float32)
    )
    result = (1.0 - update) * candidate + update * hidden.astype(jnp.float32)
    return result.astype(jnp.bfloat16).reshape(state_rows.shape)


def place_poles(tall, mirrored, band_index, band_count):
    north = jnp.where(band_index == 0, mirrored[0], tall[0])
    south = jnp.where(band_index == band_count - 1, mirrored[1], tall[-1])
    return jnp.concatenate([north[None], tall[1:-1], south[None]], axis=0)


def pad_tile(current, band_index, band_count, half_cycle):
    widened = extended(current, (("lon", 1),), 1, True)
    tall = extended(widened, (("lat", 0),), 1, False)
    mirrored = passed_along(jnp.stack([widened[0], widened[-1]]), "lon", half_cycle)
    return place_poles(tall, mirrored, band_index, band_count)


def on_device(state, edge_metric, stencil_coef, norm_gain, biases, weights):
    gathered = lax.all_gather(weights, ("lat", "lon"), axis=1, tiled=True)
    band_index = lax.axis_index("lat")
    band_count = lax.axis_size("lat")
    half_cycle = lax.axis_size("lon") // 2
    channels = state.shape[2]
    current = state
    for iteration in range(ITERS):
        padded = pad_tile(current, band_index, band_count, half_cycle)
        mats = gathered[iteration].reshape(KMAT, channels, channels)
        current = grid_update(
            padded,
            edge_metric,
            current,
            stencil_coef[iteration],
            norm_gain[iteration],
            biases[iteration],
            mats,
        )
    return current


def solution(mesh):
    in_specs = (
        P("lat", "lon", None),
        P(None, "lat", "lon"),
        P(),
        P(),
        P(),
        P(None, ("lat", "lon"), None),
    )
    out_specs = P("lat", "lon", None)
    return jax.shard_map(
        on_device, mesh=mesh, in_specs=in_specs, out_specs=out_specs, check_vma=False
    )
```

profile of v0, /device:TPU:7, one launch (start us, length us, event | category | flops | bytes accessed | tf_op | source)
XLA Modules:
  0.0 350.3 jit_solution(6598155244749161238)
XLA Ops:
  0.0 1.1 fusion.37
  1.1 4.1 %collective-permute-start = (bf16[128,1,128]{2,1,0:T(2,128)(2,1)S(1)}, bf16[128,1,128]{2,1,0:T(2,128)(2,1)S(1)}, u32[]{:S(2)}, u32[]{:S(2)}) collective-permute-start(bf16[128,1,128]{2,1,0:T(2,128)(2,1)S(1)} %get-tuple-element.19), channel_id=1, source_target_pairs={{0,1},{1,2},{2,3},{3,4},{4,5},{5,6},{6,7},{7,8},{8,9},{9,10},{10,1... | collective-permute-start | bytes 98312 | tf_op jit(solution)/shard_map/ppermute | solution.py:19
  5.3 0.0 collective-permute-start.1
  5.3 1.5 slice_bitcast_fusion.36
  6.8 1.1 slice_bitcast_fusion.8
  7.9 168.0 %all_gather.3 = bf16[2,896,128]{2,0,1:T(2,128)(2,1)S(1)} all-gather(bf16[2,7,128]{2,0,1:T(2,128)(2,1)} %param.11), channel_id=1, replica_groups=mesh['lat'=8,'lon'=16] {'lat','lon'}, dimensions={1}, use_global_device_ids=true | all-gather | bytes 462336 | tf_op jit(solution)/shard_map/all_gather | solution.py:85
  176.0 1.5 fusion.38
  177.4 1.5 slice_bitcast_fusion.11
  178.9 0.0 collective-permute-done
  178.9 0.0 collective-permute-done.1
  178.9 0.8 pad_maximum_fusion.11
  179.7 1.3 collective-permute-start.3
  181.0 0.6 pad_maximum_fusion.6
  181.6 1.3 collective-permute-start.4
  182.9 0.3 collective-permute-start.2
  183.2 0.8 slice_bitcast_fusion.13
  184.0 2.4 collective-permute-done.4
  186.4 2.2 collective-permute-done.2
  188.6 0.8 slice_select_fusion.3
  189.4 9.6 %maximum_maximum_fusion = (bf16[129,130,128]{2,1,0:T(8,128)(2,1)S(1)}, bf16[129,130,128]{2,1,0:T(8,128)(2,1)S(1)}) fusion(bf16[128,1,128]{2,1,0:T(2,128)(2,1)S(1)} %collective-permute-done.1, bf16[128,128,128]{2,1,0:T(8,128)(2,1)} %param.6, bf16[128,1,128]{2,1,0:T(2,128)(2,1)S(1)} %collective-permute-done, bf16[1,130,128]{2,1,0:T(8,128)(2,1)S(1)} %get-tuple-element.46, ...), kind=kLoop, calls=%fused_computation.48 | loop fusion | flops 34344960 | bytes 12912640 | tf_op jit(solution)/shard_map/concatenate | solution.py:74
  199.0 24.2 %multiply_reduce_fusion.1 = (f32[128,128]{1,0:T(8,128)S(1)}, f32[128,128,128]{2,1,0:T(8,128)S(1)}) fusion(bf16[129,130,128]{2,1,0:T(8,128)(2,1)S(1)} %get-tuple-element.14, f32[128]{0:T(128)} %get-tuple-element.55, f32[128,128]{1,0:T(8,128)S(1)} %get-tuple-element.28, f32[128]{0:T(128)} %get-tuple-element.56, f32[128,128]{1,0:T(8,128)S(1)} %get-tuple-element.29, ...), kind=kLoop, calls=%fused_computation.46 | loop fusion | flops 90161152 | bytes 38474240 | tf_op jit(solution)/shard_map/reduce_sum | solution.py:46
  223.3 4.7 %multiply_convert_fusion.1 = bf16[128,128,128]{2,1,0:T(8,128)(2,1)S(1)} fusion(f32[128,128,128]{2,1,0:T(8,128)S(1)} %get-tuple-element.8, f32[128]{0:T(128)S(1)} %get-tuple-element.75, f32[128,128]{1,0:T(8,128)S(1)} %add_rsqrt_fusion.1), kind=kLoop, calls=%fused_computation.45 | loop fusion | flops 6291456 | bytes 12648960 | tf_op jit(solution)/shard_map/convert_element_type | solution.py:47
  228.0 1.2 fusion.26
  229.2 1.2 fusion.35
  230.5 1.2 fusion.34
  231.7 4.5 %convolution_add_fusion.5 = f32[16384,128]{1,0:T(8,128)} fusion(bf16[16384,128]{1,0:T(8,128)(2,1)S(1)} %fusion.26, f32[128]{0:T(128)S(1)} %get-tuple-element.69, bf16[1,128,128]{2,0,1:T(2,128)(2,1)S(1)} %get-tuple-element.40), kind=kOutput, calls=%fused_computation.25 | convolution fusion | flops 538968064 | bytes 12616192 | tf_op jit(solution)/shard_map/dot_general | solution.py:63
  236.3 4.5 %fusion.28 = f32[16384,128]{1,0:T(8,128)} fusion(f32[16384,128]{1,0:T(8,128)S(1)} %fusion.35, bf16[16384,128]{1,0:T(8,128)(2,1)S(1)} %bitcast.139, f32[128]{0:T(128)S(1)} %copy-done.17, bf16[1,128,128]{2,0,1:T(2,128)(2,1)S(1)} %copy-done.4), kind=kOutput, calls=%fused_computation.38 | convolution fusion | flops 547356672 | bytes 21004800 | tf_op jit(solution)/shard_map/dot_general | solution.py:54
  240.8 4.6 %fusion.29 = f32[16384,128]{1,0:T(8,128)} fusion(f32[16384,128]{1,0:T(8,128)S(1)} %fusion.34, bf16[16384,128]{1,0:T(8,128)(2,1)S(1)} %bitcast.140, f32[128]{0:T(128)S(1)} %copy-done.16, bf16[1,128,128]{2,0,1:T(2,128)(2,1)S(1)} %copy-done.3), kind=kOutput, calls=%fused_computation.39 | convolution fusion | flops 547356672 | bytes 21004800 | tf_op jit(solution)/shard_map/dot_general | solution.py:59
  245.4 9.8 %fusion.25 = bf16[16384,128]{1,0:T(8,128)(2,1)S(1)} fusion(f32[16384,128]{1,0:T(8,128)} %convolution_add_fusion.5, f32[16384,128]{1,0:T(8,128)} %fusion.29, bf16[16384,128]{1,0:T(8,128)(2,1)S(1)} %bitcast.141, f32[16384,128]{1,0:T(8,128)} %fusion.28, bf16[1,128,128]{2,0,1:T(2,128)(2,1)S(1)} %get-tuple-element.37), kind=kOutput, calls=%fused_computation.35 | convolution fusion | flops 553648128 | bytes 33587200 | tf_op jit(solution)/shard_map/dot_general | solution.py:65
  255.2 0.1 fusion.36
  255.3 11.3 %collective-permute-start.5 = (bf16[128,1,128]{2,1,0:T(2,128)(2,1)S(1)}, bf16[128,1,128]{2,1,0:T(2,128)(2,1)S(1)}, u32[]{:S(2)}, u32[]{:S(2)}) collective-permute-start(bf16[128,1,128]{2,1,0:T(2,128)(2,1)S(1)} %get-tuple-element.17), channel_id=1, source_target_pairs={{0,1},{1,2},{2,3},{3,4},{4,5},{5,6},{6,7},{7,8},{8,9},{9,10},{10,1... | collective-permute-start | bytes 98312 | tf_op jit(solution)/shard_map/ppermute | solution.py:19
  266.7 0.1 collective-permute-start.6
  266.8 1.2 collective-permute-done.5
  268.0 6.1 %collective-permute-done.6 = bf16[128,1,128]{2,1,0:T(2,128)(2,1)S(1)} collective-permute-done((bf16[128,1,128]{2,1,0:T(2,128)(2,1)S(1)}, bf16[128,1,128]{2,1,0:T(2,128)(2,1)S(1)}, u32[]{:S(2)}, u32[]{:S(2)}) %collective-permute-start.6) | collective-permute-done | bytes 32800 | tf_op jit(solution)/shard_map/ppermute | solution.py:21
  274.1 3.0 collective-permute-start.7
  277.2 4.1 %collective-permute-start.8 = (bf16[1,130,128]{2,1,0:T(8,128)(2,1)S(1)}, bf16[1,130,128]{2,1,0:T(8,128)(2,1)S(1)}, u32[]{:S(2)}, u32[]{:S(2)}) collective-permute-start(bf16[1,130,128]{2,1,0:T(8,128)(2,1)S(1)} %get-tuple-element.11), channel_id=1, source_target_pairs={{0,16},{16,32},{32,48},{48,64},{64,80},{80,96},{96,112},{1,17},{17... | collective-permute-start | bytes 99848 | tf_op jit(solution)/shard_map/ppermute | solution.py:19
  281.3 1.3 collective-permute-start.9
  282.6 3.4 collective-permute-done.9
  286.0 6.8 %maximum_maximum_fusion.1 = (bf16[129,130,128]{2,1,0:T(8,128)(2,1)S(1)}, bf16[129,130,128]{2,1,0:T(8,128)(2,1)S(1)}) fusion(bf16[128,1,128]{2,1,0:T(2,128)(2,1)S(1)} %collective-permute-done.6, bf16[128,128,128]{2,1,0:T(8,128)(2,1)S(1)} %bitcast.137, bf16[128,1,128]{2,1,0:T(2,128)(2,1)S(1)} %collective-permute-done.5, ...), kind=kLoop, calls=%fused_computation.50 | loop fusion | flops 34344960 | bytes 12912640 | tf_op jit(solution)/shard_map/concatenate | solution.py:74
  293.0 23.4 %multiply_reduce_fusion = (f32[128,128]{1,0:T(8,128)S(1)}, f32[128,128,128]{2,1,0:T(8,128)S(1)}) fusion(bf16[129,130,128]{2,1,0:T(8,128)(2,1)S(1)} %get-tuple-element.10, f32[128]{0:T(128)S(1)} %copy-done.12, f32[128,128]{1,0:T(8,128)S(1)} %get-tuple-element.28, f32[128]{0:T(128)S(1)} %copy-done.13, f32[128,128]{1,0:T(8,128)S(1)} %get-tuple-element.29, ...), kind=kLoop, calls=%fused_computation.43 | loop fusion | flops 90161152 | bytes 38474240 | tf_op jit(solution)/shard_map/reduce_sum | solution.py:46
  316.4 4.7 %multiply_convert_fusion = bf16[128,128,128]{2,1,0:T(8,128)(2,1)S(1)} fusion(f32[128,128,128]{2,1,0:T(8,128)S(1)} %get-tuple-element.6, f32[128]{0:T(128)S(1)} %get-tuple-element.74, f32[128,128]{1,0:T(8,128)S(1)} %add_rsqrt_fusion), kind=kLoop, calls=%fused_computation.42 | loop fusion | flops 6291456 | bytes 12648960 | tf_op jit(solution)/shard_map/convert_element_type | solution.py:47
  321.1 1.2 fusion.27
  322.3 1.2 fusion.33
  323.6 1.2 fusion.32
  324.8 4.5 %convolution_add_fusion.1 = f32[16384,128]{1,0:T(8,128)} fusion(bf16[16384,128]{1,0:T(8,128)(2,1)S(1)} %fusion.27, f32[128]{0:T(128)S(1)} %get-tuple-element.73, bf16[1,128,128]{2,0,1:T(2,128)(2,1)S(1)} %get-tuple-element.33), kind=kOutput, calls=%fused_computation.9 | convolution fusion | flops 538968064 | bytes 12616192 | tf_op jit(solution)/shard_map/dot_general | solution.py:63
  329.4 4.5 %fusion.30 = f32[16384,128]{1,0:T(8,128)} fusion(f32[16384,128]{1,0:T(8,128)S(1)} %fusion.33, bf16[16384,128]{1,0:T(8,128)(2,1)S(1)} %fusion.25, f32[128]{0:T(128)S(1)} %copy-done.15, bf16[1,128,128]{2,0,1:T(2,128)(2,1)S(1)} %copy-done.2), kind=kOutput, calls=%fused_computation.40 | convolution fusion | flops 547356672 | bytes 21004800 | tf_op jit(solution)/shard_map/dot_general | solution.py:54
  333.9 4.6 %fusion.31 = f32[16384,128]{1,0:T(8,128)} fusion(f32[16384,128]{1,0:T(8,128)S(1)} %fusion.32, bf16[16384,128]{1,0:T(8,128)(2,1)S(1)} %fusion.25, f32[128]{0:T(128)S(1)} %copy-done.14, bf16[1,128,128]{2,0,1:T(2,128)(2,1)S(1)} %copy-done.1), kind=kOutput, calls=%fused_computation.41 | convolution fusion | flops 547356672 | bytes 21004800 | tf_op jit(solution)/shard_map/dot_general | solution.py:59
  338.5 11.8 %fusion.24 = bf16[16384,128]{1,0:T(8,128)(2,1)} fusion(f32[16384,128]{1,0:T(8,128)} %convolution_add_fusion.1, f32[16384,128]{1,0:T(8,128)} %fusion.31, bf16[16384,128]{1,0:T(8,128)(2,1)S(1)} %fusion.25, f32[16384,128]{1,0:T(8,128)} %fusion.30, bf16[1,128,128]{2,0,1:T(2,128)(2,1)S(1)} %get-tuple-element.30), kind=kOutput, calls=%fused_computation.34 | convolution fusion | flops 553648128 | bytes 33587200 | tf_op jit(solution)/shard_map/dot_general | solution.py:65
  (44 shorter events, 0.2 us)
Async XLA Ops:
  1.1 177.7 %collective-permute-start = (bf16[128,1,128]{2,1,0:T(2,128)(2,1)S(1)}, bf16[128,1,128]{2,1,0:T(2,128)(2,1)S(1)}, u32[]{:S(2)}, u32[]{:S(2)}) collective-permute-start(bf16[128,1,128]{2,1,0:T(2,128)(2,1)S(1)} %get-tuple-element.19), channel_id=1, source_target_pairs={{0,1},{1,2},{2,3},{3,4},{4,5},{5,6},{6,7},{7,8},{8,9},{9,10},{10,1... | collective-permute-start | bytes 98312 | tf_op jit(solution)/shard_map/ppermute | solution.py:19
  5.3 173.6 %collective-permute-start.1 = (bf16[128,1,128]{2,1,0:T(2,128)(2,1)S(1)}, bf16[128,1,128]{2,1,0:T(2,128)(2,1)S(1)}, u32[]{:S(2)}, u32[]{:S(2)}) collective-permute-start(bf16[128,1,128]{2,1,0:T(2,128)(2,1)S(1)} %get-tuple-element.20), channel_id=1, source_target_pairs={{1,0},{2,1},{3,2},{4,3},{5,4},{6,5},{7,6},{8,7},{9,8},{10,9},{11,1... | collective-permute-start | bytes 98312 | tf_op jit(solution)/shard_map/ppermute | solution.py:21
  179.7 4.3 %collective-permute-start.3 = (bf16[1,130,128]{2,1,0:T(8,128)(2,1)S(1)}, bf16[1,130,128]{2,1,0:T(8,128)(2,1)S(1)}, u32[]{:S(2)}, u32[]{:S(2)}) collective-permute-start(bf16[1,130,128]{2,1,0:T(8,128)(2,1)S(1)} %get-tuple-element.15), channel_id=1, source_target_pairs={{0,16},{16,32},{32,48},{48,64},{64,80},{80,96},{96,112},{1,17},{17... | collective-permute-start | bytes 99848 | tf_op jit(solution)/shard_map/ppermute | solution.py:19
  181.6 4.8 %collective-permute-start.4 = (bf16[1,130,128]{2,1,0:T(8,128)(2,1)S(1)}, bf16[1,130,128]{2,1,0:T(8,128)(2,1)}, u32[]{:S(2)}, u32[]{:S(2)}) collective-permute-start(bf16[1,130,128]{2,1,0:T(8,128)(2,1)S(1)} %get-tuple-element.16), channel_id=1, source_target_pairs={{16,0},{32,16},{48,32},{64,48},{80,64},{96,80},{112,96},{17,1},{33... | collective-permute-start | bytes 99848 | tf_op jit(solution)/shard_map/ppermute | solution.py:21
  182.9 5.7 %collective-permute-start.2 = (bf16[2,130,128]{2,1,0:T(8,128)(2,1)}, bf16[2,130,128]{2,1,0:T(8,128)(2,1)}, u32[]{:S(2)}, u32[]{:S(2)}) collective-permute-start(bf16[2,130,128]{2,1,0:T(8,128)(2,1)} %pad_maximum_fusion.6), channel_id=1, source_target_pairs={{8,0},{9,1},{10,2},{11,3},{12,4},{13,5},{14,6},{15,7},{0,8},{1,9},... | collective-permute-start | bytes 199688 | tf_op jit(solution)/shard_map/ppermute | solution.py:31
  184.0 15.0 %copy-start = (bf16[128,128,128]{2,1,0:T(8,128)(2,1)S(1)}, bf16[128,128,128]{2,1,0:T(8,128)(2,1)}, u32[]{:S(2)}) copy-start(bf16[128,128,128]{2,1,0:T(8,128)(2,1)} %param.6) | copy-start | bytes 12582916
  231.7 4.5 %copy-start.4 = (bf16[1,128,128]{2,0,1:T(2,128)(2,1)S(1)}, bf16[1,128,128]{2,0,1:T(2,128)(2,1)}, u32[]{:S(2)}) copy-start(bf16[1,128,128]{2,0,1:T(2,128)(2,1)} %get-tuple-element.41) | copy-start | bytes 98308
  231.7 4.5 %copy-start.17 = (f32[128]{0:T(128)S(1)}, f32[128]{0:T(128)}, u32[]{:S(2)}) copy-start(f32[128]{0:T(128)} %get-tuple-element.70) | copy-start | bytes 1540
  236.3 4.6 %copy-start.3 = (bf16[1,128,128]{2,0,1:T(2,128)(2,1)S(1)}, bf16[1,128,128]{2,0,1:T(2,128)(2,1)}, u32[]{:S(2)}) copy-start(bf16[1,128,128]{2,0,1:T(2,128)(2,1)} %get-tuple-element.38) | copy-start | bytes 98308
  236.3 4.6 %copy-start.16 = (f32[128]{0:T(128)S(1)}, f32[128]{0:T(128)}, u32[]{:S(2)}) copy-start(f32[128]{0:T(128)} %get-tuple-element.68) | copy-start | bytes 1540
  255.3 12.7 %collective-permute-start.5 = (bf16[128,1,128]{2,1,0:T(2,128)(2,1)S(1)}, bf16[128,1,128]{2,1,0:T(2,128)(2,1)S(1)}, u32[]{:S(2)}, u32[]{:S(2)}) collective-permute-start(bf16[128,1,128]{2,1,0:T(2,128)(2,1)S(1)} %get-tuple-element.17), channel_id=1, source_target_pairs={{0,1},{1,2},{2,3},{3,4},{4,5},{5,6},{6,7},{7,8},{8,9},{9,10},{10,1... | collective-permute-start | bytes 98312 | tf_op jit(solution)/shard_map/ppermute | solution.py:19
  266.6 26.2 %copy-start.5 = (f32[128]{0:T(128)S(1)}, f32[128]{0:T(128)}, u32[]{:S(2)}) copy-start(f32[128]{0:T(128)} %get-tuple-element.48) | copy-start | bytes 1540
  266.6 26.3 %copy-start.6 = (f32[128]{0:T(128)S(1)}, f32[128]{0:T(128)}, u32[]{:S(2)}) copy-start(f32[128]{0:T(128)} %get-tuple-element.49) | copy-start | bytes 1540
  266.6 26.3 %copy-start.7 = (f32[128]{0:T(128)S(1)}, f32[128]{0:T(128)}, u32[]{:S(2)}) copy-start(f32[128]{0:T(128)} %get-tuple-element.50) | copy-start | bytes 1540
  266.6 26.3 %copy-start.8 = (f32[128]{0:T(128)S(1)}, f32[128]{0:T(128)}, u32[]{:S(2)}) copy-start(f32[128]{0:T(128)} %get-tuple-element.51) | copy-start | bytes 1540
  266.6 26.3 %copy-start.9 = (f32[128]{0:T(128)S(1)}, f32[128]{0:T(128)}, u32[]{:S(2)}) copy-start(f32[128]{0:T(128)} %get-tuple-element.52) | copy-start | bytes 1540
  266.7 26.3 %copy-start.10 = (f32[128]{0:T(128)S(1)}, f32[128]{0:T(128)}, u32[]{:S(2)}) copy-start(f32[128]{0:T(128)} %get-tuple-element.53) | copy-start | bytes 1540
  266.7 26.3 %copy-start.11 = (f32[128]{0:T(128)S(1)}, f32[128]{0:T(128)}, u32[]{:S(2)}) copy-start(f32[128]{0:T(128)} %get-tuple-element.54) | copy-start | bytes 1540
  266.7 26.3 %copy-start.12 = (f32[128]{0:T(128)S(1)}, f32[128]{0:T(128)}, u32[]{:S(2)}) copy-start(f32[128]{0:T(128)} %get-tuple-element.64) | copy-start | bytes 1540
  266.7 26.3 %copy-start.13 = (f32[128]{0:T(128)S(1)}, f32[128]{0:T(128)}, u32[]{:S(2)}) copy-start(f32[128]{0:T(128)} %get-tuple-element.65) | copy-start | bytes 1540
  266.7 7.4 %collective-permute-start.6 = (bf16[128,1,128]{2,1,0:T(2,128)(2,1)S(1)}, bf16[128,1,128]{2,1,0:T(2,128)(2,1)S(1)}, u32[]{:S(2)}, u32[]{:S(2)}) collective-permute-start(bf16[128,1,128]{2,1,0:T(2,128)(2,1)S(1)} %get-tuple-element.18), channel_id=1, source_target_pairs={{1,0},{2,1},{3,2},{4,3},{5,4},{6,5},{7,6},{8,7},{9,8},{10,9},{11,1... | collective-permute-start | bytes 98312 | tf_op jit(solution)/shard_map/ppermute | solution.py:21
  274.1 11.9 %collective-permute-start.7 = (bf16[2,130,128]{2,1,0:T(8,128)(2,1)S(1)}, bf16[2,130,128]{2,1,0:T(8,128)(2,1)S(1)}, u32[]{:S(2)}, u32[]{:S(2)}) collective-permute-start(bf16[2,130,128]{2,1,0:T(8,128)(2,1)S(1)} %pad_maximum_fusion.7), channel_id=1, source_target_pairs={{8,0},{9,1},{10,2},{11,3},{12,4},{13,5},{14,6},{15,7},{0,8},{1,9},... | collective-permute-start | bytes 199688 | tf_op jit(solution)/shard_map/ppermute | solution.py:31
  277.2 5.5 %collective-permute-start.8 = (bf16[1,130,128]{2,1,0:T(8,128)(2,1)S(1)}, bf16[1,130,128]{2,1,0:T(8,128)(2,1)S(1)}, u32[]{:S(2)}, u32[]{:S(2)}) collective-permute-start(bf16[1,130,128]{2,1,0:T(8,128)(2,1)S(1)} %get-tuple-element.11), channel_id=1, source_target_pairs={{0,16},{16,32},{32,48},{48,64},{64,80},{80,96},{96,112},{1,17},{17... | collective-permute-start | bytes 99848 | tf_op jit(solution)/shard_map/ppermute | solution.py:19
  281.3 4.7 %collective-permute-start.9 = (bf16[1,130,128]{2,1,0:T(8,128)(2,1)S(1)}, bf16[1,130,128]{2,1,0:T(8,128)(2,1)S(1)}, u32[]{:S(2)}, u32[]{:S(2)}) collective-permute-start(bf16[1,130,128]{2,1,0:T(8,128)(2,1)S(1)} %get-tuple-element.12), channel_id=1, source_target_pairs={{16,0},{32,16},{48,32},{64,48},{80,64},{96,80},{112,96},{17,1},{33... | collective-permute-start | bytes 99848 | tf_op jit(solution)/shard_map/ppermute | solution.py:21
  324.8 4.5 %copy-start.2 = (bf16[1,128,128]{2,0,1:T(2,128)(2,1)S(1)}, bf16[1,128,128]{2,0,1:T(2,128)(2,1)}, u32[]{:S(2)}) copy-start(bf16[1,128,128]{2,0,1:T(2,128)(2,1)} %get-tuple-element.34) | copy-start | bytes 98308
  324.8 4.5 %copy-start.15 = (f32[128]{0:T(128)S(1)}, f32[128]{0:T(128)}, u32[]{:S(2)}) copy-start(f32[128]{0:T(128)} %get-tuple-element.66) | copy-start | bytes 1540
  329.4 4.6 %copy-start.1 = (bf16[1,128,128]{2,0,1:T(2,128)(2,1)S(1)}, bf16[1,128,128]{2,0,1:T(2,128)(2,1)}, u32[]{:S(2)}) copy-start(bf16[1,128,128]{2,0,1:T(2,128)(2,1)} %get-tuple-element.31) | copy-start | bytes 98308
  329.4 4.6 %copy-start.14 = (f32[128]{0:T(128)S(1)}, f32[128]{0:T(128)}, u32[]{:S(2)}) copy-start(f32[128]{0:T(128)} %get-tuple-element.72) | copy-start | bytes 1540
where the time goes:
time: 351 us; the launch traced here: 350 us
  blocking collectives  168 us (48%)
  other arithmetic  75.8 us (22%)
  matrix products  56.3 us (16%)
  starting transfers between devices  26.9 us (8%)
  waiting for transfers between devices  15.3 us (4%)
  local copies, waits for them, and re-layouts  7.64 us (2%)
    all_gather x1, blocking collectives, on_device(): gathered = lax.all_gather(weights, ('lat', 'lon'), axis=1, tiled=True)  168 us
    reduce_sum x2, other arithmetic, grid_update(): jnp.mean(summed * summed, axis=-1, keepdims=True) + EPSILON  47.6 us
    dot_general x2, matrix products, grid_update(): jnp.dot(hidden, mats[6], preferred_element_type=jnp.float32)  21.6 us
    ppermute x4, starting transfers between devices, extended(): lax.ppermute(tail, axis, [(i, (i + 1) % count) for i in range(ends)])  20.9 us
    concatenate x2, other arithmetic, place_poles(): return jnp.concatenate([north[None], tall[1:-1], south[None]], axis=0)  16.4 us
    ppermute x4, waiting for transfers between devices, extended(): lax.ppermute(head, axis, [((i + 1) % count, i) for i in range(ends)])  11.9 us
    convert_element_type x2, other arithmetic, grid_update(): normed = (summed * scale * gain).astype(jnp.bfloat16).reshape(-1, channels)  9.45 us
    dot_general x2, matrix products, grid_update(): jnp.dot(hidden, mats[5], preferred_element_type=jnp.float32)  9.18 us
  transfers between devices with their start and end apart: 10, of which 5 were waited for; matrix products, arithmetic and copies ran while one was open for 2% of the time, Pallas kernels for 0%

commit v1 on v0

--- a/solution.py
+++ b/solution.py
@@ -82,7 +82,10 @@
 
 
 def on_device(state, edge_metric, stencil_coef, norm_gain, biases, weights):
-    gathered = lax.all_gather(weights, ("lat", "lon"), axis=1, tiled=True)
+    gathered = jnp.concatenate(
+        lax.all_to_all(jnp.stack([weights] * lax.axis_size(("lat", "lon"))), ("lat", "lon"), 0, 0),
+        axis=1,
+    )
     band_index = lax.axis_index("lat")
     band_count = lax.axis_size("lat")
     half_cycle = lax.axis_size("lon") // 2

time: 351 us -> 190 us (0.54)
  blocking collectives: 168 us -> 0 us
  starting transfers between devices: 26.9 us -> 31.8 us
    all_gather x1 -> x0, blocking collectives: 168 us -> none  [on_device(): gathered = lax.all_gather(weights, ('lat', 'lon'), axis=1, tiled=True)]
    all_to_all x0 -> x1, starting transfers between devices: none -> 9.58 us  [on_device(): lax.all_to_all(jnp.stack([weights] * lax.axis_size(('lat', 'lon'))), ('la...]
    ppermute x4, starting transfers between devices: 20.9 us -> 16.5 us  [extended(): lax.ppermute(tail, axis, [(i, (i + 1) % count) for i in range(ends)])]
  transfers between devices with their start and end apart: 10 -> 11, of which waited for: 5 -> 4; matrix products, arithmetic and copies ran while one was open for 2% -> 23% of each run, Pallas kernels for 0% -> 0%
where the time goes in v1:
time: 190 us; the launch traced here: 188 us
  other arithmetic  76 us (40%)
  matrix products  58.3 us (31%)
  starting transfers between devices  31.8 us (17%)
  waiting for transfers between devices  12.3 us (6%)
  local copies, waits for them, and re-layouts  9.2 us (5%)
    reduce_sum x2, other arithmetic, grid_update(): jnp.mean(summed * summed, axis=-1, keepdims=True) + EPSILON  46.7 us
    dot_general x2, matrix products, grid_update(): jnp.dot(hidden, mats[6], preferred_element_type=jnp.float32)  21.6 us
    concatenate x2, other arithmetic, place_poles(): return jnp.concatenate([north[None], tall[1:-1], south[None]], axis=0)  19.2 us
    ppermute x4, starting transfers between devices, extended(): lax.ppermute(tail, axis, [(i, (i + 1) % count) for i in range(ends)])  16.5 us
    ppermute x4, waiting for transfers between devices, extended(): lax.ppermute(head, axis, [((i + 1) % count, i) for i in range(ends)])  9.95 us
    all_to_all x1, starting transfers between devices, on_device(): lax.all_to_all(jnp.stack([weights] * lax.axis_size(('lat', 'lon'))), ('la...  9.58 us
    dot_general x2, matrix products, grid_update(): jnp.dot(hidden, mats[4], preferred_element_type=jnp.float32)  9.09 us
    convert_element_type x2, other arithmetic, grid_update(): normed = (summed * scale * gain).astype(jnp.bfloat16).reshape(-1, channels)  9.06 us
  transfers between devices with their start and end apart: 11, of which 4 were waited for; matrix products, arithmetic and copies ran while one was open for 23% of the time, Pallas kernels for 0%

profile of v1, /device:TPU:7, one launch (start us, length us, event | category | flops | bytes accessed | tf_op | source)
XLA Modules:
  0.0 187.8 jit_solution(7713991925421806236)
XLA Ops:
  0.0 1.1 fusion.37
  1.1 4.1 %collective-permute-start = (bf16[128,1,128]{2,1,0:T(2,128)(2,1)S(1)}, bf16[128,1,128]{2,1,0:T(2,128)(2,1)S(1)}, u32[]{:S(2)}, u32[]{:S(2)}) collective-permute-start(bf16[128,1,128]{2,1,0:T(2,128)(2,1)S(1)} %get-tuple-element.21), channel_id=1, source_target_pairs={{0,1},{1,2},{2,3},{3,4},{4,5},{5,6},{6,7},{7,8},{8,9},{9,10},{10,1... | collective-permute-start | bytes 98312 | tf_op jit(solution)/shard_map/ppermute | solution.py:19
  5.3 0.0 collective-permute-start.1
  5.3 1.7 stack.7
  7.0 9.6 %all-to-all-start = ((bf16[128,2,7,128]{3,1,2,0:T(2,128)(2,1)}), bf16[128,2,7,128]{3,1,2,0:T(2,128)(2,1)S(1)}, u32[]{:S(2)}, u32[]{:S(2)}) async-start(bf16[128,2,7,128]{3,1,2,0:T(2,128)(2,1)} %stack.7), calls=%async_computation | async-start | bytes 917504 | tf_op jit(solution)/shard_map/all_to_all | solution.py:86
  16.6 0.9 slice_bitcast_fusion.64
  17.4 1.1 slice_bitcast_fusion.8
  18.6 0.9 slice_bitcast_fusion.39
  19.5 0.8 pad_maximum_fusion.11
  20.3 3.3 %collective-permute-start.3 = (bf16[1,130,128]{2,1,0:T(8,128)(2,1)S(1)}, bf16[1,130,128]{2,1,0:T(8,128)(2,1)S(1)}, u32[]{:S(2)}, u32[]{:S(2)}) collective-permute-start(bf16[1,130,128]{2,1,0:T(8,128)(2,1)S(1)} %get-tuple-element.17), channel_id=1, source_target_pairs={{0,16},{16,32},{32,48},{48,64},{64,80},{80,96},{96,112},{1,17},{17... | collective-permute-start | bytes 99848 | tf_op jit(solution)/shard_map/ppermute | solution.py:19
  23.6 1.3 collective-permute-start.4
  24.9 3.0 %collective-permute-start.2 = (bf16[2,130,128]{2,1,0:T(8,128)(2,1)S(1)}, bf16[2,130,128]{2,1,0:T(8,128)(2,1)S(1)}, u32[]{:S(2)}, u32[]{:S(2)}) collective-permute-start(bf16[2,130,128]{2,1,0:T(8,128)(2,1)S(1)} %pad_maximum_fusion.6), channel_id=1, source_target_pairs={{8,0},{9,1},{10,2},{11,3},{12,4},{13,5},{14,6},{15,7},{0,8},{1,9},... | collective-permute-start | bytes 199688 | tf_op jit(solution)/shard_map/ppermute | solution.py:31
  27.9 0.8 slice_bitcast_fusion.41
  28.7 1.0 collective-permute-done.2
  29.6 9.6 %maximum_maximum_fusion = (bf16[129,130,128]{2,1,0:T(8,128)(2,1)S(1)}, bf16[129,130,128]{2,1,0:T(8,128)(2,1)S(1)}) fusion(bf16[128,1,128]{2,1,0:T(2,128)(2,1)S(1)} %collective-permute-done.1, bf16[128,128,128]{2,1,0:T(8,128)(2,1)} %param.6, bf16[128,1,128]{2,1,0:T(2,128)(2,1)S(1)} %collective-permute-done, bf16[1,130,128]{2,1,0:T(8,128)(2,1)S(1)} %get-tuple-element.34, ...), kind=kLoop, calls=%fused_computation.48 | loop fusion | flops 34344960 | bytes 12912640 | tf_op jit(solution)/shard_map/concatenate | solution.py:74
  39.2 23.4 %multiply_reduce_fusion.1 = (f32[128,128]{1,0:T(8,128)S(1)}, f32[128,128,128]{2,1,0:T(8,128)S(1)}) fusion(bf16[129,130,128]{2,1,0:T(8,128)(2,1)S(1)} %get-tuple-element.16, f32[128]{0:T(128)S(1)} %get-tuple-element.43, f32[128,128]{1,0:T(8,128)S(1)} %get-tuple-element.30, f32[128]{0:T(128)S(1)} %get-tuple-element.44, f32[128,128]{1,0:T(8,128)S(1)} %get-tuple-element.31, ...), kind=kLoop, calls=%fused_computation.46 | loop fusion | flops 90161152 | bytes 38474240 | tf_op jit(solution)/shard_map/reduce_sum | solution.py:46
  62.7 4.3 %multiply_convert_fusion.1 = bf16[128,128,128]{2,1,0:T(8,128)(2,1)} fusion(f32[128,128,128]{2,1,0:T(8,128)S(1)} %get-tuple-element.10, f32[128]{0:T(128)S(1)} %get-tuple-element.63, f32[128,128]{1,0:T(8,128)S(1)} %add_rsqrt_fusion.1), kind=kLoop, calls=%fused_computation.45 | loop fusion | flops 6291456 | bytes 12648960 | tf_op jit(solution)/shard_map/convert_element_type | solution.py:47
  67.0 2.4 %slice_reduce_fusion = (bf16[128,7,128]{2,1,0:T(8,128)(2,1)S(1)}, bf16[128,7,128]{2,1,0:T(8,128)(2,1)S(1)}) fusion(bf16[2,128,7,128]{3,0,2,1:T(2,128)(2,1)S(1)} %bitcast.145), kind=kLoop, calls=%fused_computation.56 | loop fusion | bytes 917504 | tf_op jit(solution)/shard_map/slice | solution.py:96
  69.4 0.1 reshape_squeeze.6
  69.5 3.4 %fusion.26 = bf16[16384,128]{1,0:T(8,128)(2,1)S(1)} fusion(bf16[16384,128]{1,0:T(8,128)(2,1)} %bitcast.143, f32[128]{0:T(128)S(1)} %get-tuple-element.59, bf16[7,128,128]{2,1,0:T(8,128)(2,1)S(1)} %reshape_squeeze.6), kind=kOutput, calls=%fused_computation.36 | convolution fusion | flops 541065216 | bytes 8421888 | tf_op jit(solution)/shard_map/dot_general | solution.py:49
  73.0 1.2 fusion.34
  74.2 1.2 fusion.35
  75.4 0.0 copy-start.3
  75.4 4.5 %convolution_add_fusion.5 = f32[16384,128]{1,0:T(8,128)} fusion(bf16[16384,128]{1,0:T(8,128)(2,1)S(1)} %fusion.26, f32[128]{0:T(128)S(1)} %get-tuple-element.57, bf16[7,128,128]{2,1,0:T(8,128)(2,1)S(1)} %reshape_squeeze.6), kind=kOutput, calls=%fused_computation.25 | convolution fusion | flops 538968064 | bytes 12616192 | tf_op jit(solution)/shard_map/dot_general | solution.py:63
  79.9 4.5 %fusion.29 = f32[16384,128]{1,0:T(8,128)} fusion(f32[16384,128]{1,0:T(8,128)S(1)} %fusion.34, bf16[16384,128]{1,0:T(8,128)(2,1)S(1)} %bitcast.140, f32[128]{0:T(128)S(1)} %get-tuple-element.56, bf16[7,128,128]{2,1,0:T(8,128)(2,1)S(1)} %reshape_squeeze.6), kind=kOutput, calls=%fused_computation.39 | convolution fusion | flops 547356672 | bytes 21004800 | tf_op jit(solution)/shard_map/dot_general | solution.py:59
  84.4 4.6 %fusion.28 = f32[16384,128]{1,0:T(8,128)} fusion(f32[16384,128]{1,0:T(8,128)S(1)} %fusion.35, bf16[16384,128]{1,0:T(8,128)(2,1)S(1)} %bitcast.141, f32[128]{0:T(128)S(1)} %get-tuple-element.58, bf16[7,128,128]{2,1,0:T(8,128)(2,1)S(1)} %reshape_squeeze.6), kind=kOutput, calls=%fused_computation.38 | convolution fusion | flops 547356672 | bytes 21004800 | tf_op jit(solution)/shard_map/dot_general | solution.py:54
  89.0 9.8 %fusion.25 = bf16[16384,128]{1,0:T(8,128)(2,1)S(1)} fusion(f32[16384,128]{1,0:T(8,128)} %convolution_add_fusion.5, f32[16384,128]{1,0:T(8,128)} %fusion.29, bf16[16384,128]{1,0:T(8,128)(2,1)S(1)} %bitcast.142, f32[16384,128]{1,0:T(8,128)} %fusion.28, bf16[7,128,128]{2,1,0:T(8,128)(2,1)S(1)} %reshape_squeeze.6), kind=kOutput, calls=%fused_computation.35 | convolution fusion | flops 553648128 | bytes 37781504 | tf_op jit(solution)/shard_map/dot_general | solution.py:65
  98.8 0.0 copy-start
  98.8 0.1 fusion.36
  98.9 4.6 %collective-permute-start.5 = (bf16[128,1,128]{2,1,0:T(2,128)(2,1)S(1)}, bf16[128,1,128]{2,1,0:T(2,128)(2,1)S(1)}, u32[]{:S(2)}, u32[]{:S(2)}) collective-permute-start(bf16[128,1,128]{2,1,0:T(2,128)(2,1)S(1)} %get-tuple-element.19), channel_id=1, source_target_pairs={{0,1},{1,2},{2,3},{3,4},{4,5},{5,6},{6,7},{7,8},{8,9},{9,10},{10,1... | collective-permute-start | bytes 98312 | tf_op jit(solution)/shard_map/ppermute | solution.py:19
  103.5 1.3 collective-permute-done.5
  104.9 6.0 %collective-permute-done.6 = bf16[128,1,128]{2,1,0:T(2,128)(2,1)S(1)} collective-permute-done((bf16[128,1,128]{2,1,0:T(2,128)(2,1)S(1)}, bf16[128,1,128]{2,1,0:T(2,128)(2,1)S(1)}, u32[]{:S(2)}, u32[]{:S(2)}) %collective-permute-start.6) | collective-permute-done | bytes 32800 | tf_op jit(solution)/shard_map/ppermute | solution.py:21
  110.9 0.1 collective-permute-start.7
  111.0 4.5 %collective-permute-start.8 = (bf16[1,130,128]{2,1,0:T(8,128)(2,1)S(1)}, bf16[1,130,128]{2,1,0:T(8,128)(2,1)S(1)}, u32[]{:S(2)}, u32[]{:S(2)}) collective-permute-start(bf16[1,130,128]{2,1,0:T(8,128)(2,1)S(1)} %get-tuple-element.13), channel_id=1, source_target_pairs={{0,16},{16,32},{32,48},{48,64},{64,80},{80,96},{96,112},{1,17},{17... | collective-permute-start | bytes 99848 | tf_op jit(solution)/shard_map/ppermute | solution.py:19
  115.5 1.3 collective-permute-start.9
  116.8 0.1 reshape_squeeze.7
  116.9 0.0 copy-start.1
  116.9 4.0 %collective-permute-done.9 = bf16[1,130,128]{2,1,0:T(8,128)(2,1)S(1)} collective-permute-done((bf16[1,130,128]{2,1,0:T(8,128)(2,1)S(1)}, bf16[1,130,128]{2,1,0:T(8,128)(2,1)S(1)}, u32[]{:S(2)}, u32[]{:S(2)}) %collective-permute-start.9) | collective-permute-done | bytes 33312 | tf_op jit(solution)/shard_map/ppermute | solution.py:21
  120.9 9.7 %maximum_maximum_fusion.1 = (bf16[129,130,128]{2,1,0:T(8,128)(2,1)S(1)}, bf16[129,130,128]{2,1,0:T(8,128)(2,1)S(1)}) fusion(bf16[128,1,128]{2,1,0:T(2,128)(2,1)S(1)} %collective-permute-done.6, bf16[128,128,128]{2,1,0:T(8,128)(2,1)} %bitcast.138, bf16[128,1,128]{2,1,0:T(2,128)(2,1)S(1)} %collective-permute-done.5, ...), kind=kLoop, calls=%fused_computation.50 | loop fusion | flops 34344960 | bytes 12912640 | tf_op jit(solution)/shard_map/concatenate | solution.py:74
  130.6 23.3 %multiply_reduce_fusion = (f32[128,128]{1,0:T(8,128)S(1)}, f32[128,128,128]{2,1,0:T(8,128)S(1)}) fusion(bf16[129,130,128]{2,1,0:T(8,128)(2,1)S(1)} %get-tuple-element.12, f32[128]{0:T(128)S(1)} %get-tuple-element.52, f32[128,128]{1,0:T(8,128)S(1)} %get-tuple-element.30, f32[128]{0:T(128)S(1)} %get-tuple-element.53, f32[128,128]{1,0:T(8,128)S(1)} %get-tuple-element.31, ...), kind=kLoop, calls=%fused_computation.43 | loop fusion | flops 90161152 | bytes 38474240 | tf_op jit(solution)/shard_map/reduce_sum | solution.py:46
  154.0 4.7 %multiply_convert_fusion = bf16[128,128,128]{2,1,0:T(8,128)(2,1)S(1)} fusion(f32[128,128,128]{2,1,0:T(8,128)S(1)} %get-tuple-element.8, f32[128]{0:T(128)S(1)} %get-tuple-element.62, f32[128,128]{1,0:T(8,128)S(1)} %add_rsqrt_fusion), kind=kLoop, calls=%fused_computation.42 | loop fusion | flops 6291456 | bytes 12648960 | tf_op jit(solution)/shard_map/convert_element_type | solution.py:47
  158.7 1.2 fusion.27
  160.0 1.2 fusion.32
  161.2 1.2 fusion.33
  162.4 4.5 %convolution_add_fusion.1 = f32[16384,128]{1,0:T(8,128)} fusion(bf16[16384,128]{1,0:T(8,128)(2,1)S(1)} %fusion.27, f32[128]{0:T(128)S(1)} %get-tuple-element.61, bf16[7,128,128]{2,1,0:T(8,128)(2,1)S(1)} %reshape_squeeze.7), kind=kOutput, calls=%fused_computation.9 | convolution fusion | flops 538968064 | bytes 12616192 | tf_op jit(solution)/shard_map/dot_general | solution.py:63
  166.9 4.5 %fusion.31 = f32[16384,128]{1,0:T(8,128)} fusion(f32[16384,128]{1,0:T(8,128)S(1)} %fusion.32, bf16[16384,128]{1,0:T(8,128)(2,1)S(1)} %copy-done.1, f32[128]{0:T(128)S(1)} %get-tuple-element.60, bf16[7,128,128]{2,1,0:T(8,128)(2,1)S(1)} %reshape_squeeze.7), kind=kOutput, calls=%fused_computation.41 | convolution fusion | flops 547356672 | bytes 21004800 | tf_op jit(solution)/shard_map/dot_general | solution.py:59
  171.4 4.5 %fusion.30 = f32[16384,128]{1,0:T(8,128)} fusion(f32[16384,128]{1,0:T(8,128)S(1)} %fusion.33, bf16[16384,128]{1,0:T(8,128)(2,1)S(1)} %copy-done.1, f32[128]{0:T(128)S(1)} %get-tuple-element.54, bf16[7,128,128]{2,1,0:T(8,128)(2,1)S(1)} %reshape_squeeze.7), kind=kOutput, calls=%fused_computation.40 | convolution fusion | flops 547356672 | bytes 21004800 | tf_op jit(solution)/shard_map/dot_general | solution.py:54
  176.0 11.8 %fusion.24 = bf16[16384,128]{1,0:T(8,128)(2,1)} fusion(f32[16384,128]{1,0:T(8,128)} %convolution_add_fusion.1, f32[16384,128]{1,0:T(8,128)} %fusion.31, bf16[16384,128]{1,0:T(8,128)(2,1)S(1)} %copy-done.1, f32[16384,128]{1,0:T(8,128)} %fusion.30, bf16[7,128,128]{2,1,0:T(8,128)(2,1)S(1)} %reshape_squeeze.7), kind=kOutput, calls=%fused_computation.34 | convolution fusion | flops 553648128 | bytes 37781504 | tf_op jit(solution)/shard_map/dot_general | solution.py:65
  (20 shorter events, 0.2 us)
Async XLA Ops:
  1.1 18.3 %collective-permute-start = (bf16[128,1,128]{2,1,0:T(2,128)(2,1)S(1)}, bf16[128,1,128]{2,1,0:T(2,128)(2,1)S(1)}, u32[]{:S(2)}, u32[]{:S(2)}) collective-permute-start(bf16[128,1,128]{2,1,0:T(2,128)(2,1)S(1)} %get-tuple-element.21), channel_id=1, source_target_pairs={{0,1},{1,2},{2,3},{3,4},{4,5},{5,6},{6,7},{7,8},{8,9},{9,10},{10,1... | collective-permute-start | bytes 98312 | tf_op jit(solution)/shard_map/ppermute | solution.py:19
  5.3 14.2 %collective-permute-start.1 = (bf16[128,1,128]{2,1,0:T(2,128)(2,1)S(1)}, bf16[128,1,128]{2,1,0:T(2,128)(2,1)S(1)}, u32[]{:S(2)}, u32[]{:S(2)}) collective-permute-start(bf16[128,1,128]{2,1,0:T(2,128)(2,1)S(1)} %get-tuple-element.22), channel_id=1, source_target_pairs={{1,0},{2,1},{3,2},{4,3},{5,4},{6,5},{7,6},{8,7},{9,8},{10,9},{11,1... | collective-permute-start | bytes 98312 | tf_op jit(solution)/shard_map/ppermute | solution.py:21
  7.0 60.0 %all-to-all-start = ((bf16[128,2,7,128]{3,1,2,0:T(2,128)(2,1)}), bf16[128,2,7,128]{3,1,2,0:T(2,128)(2,1)S(1)}, u32[]{:S(2)}, u32[]{:S(2)}) async-start(bf16[128,2,7,128]{3,1,2,0:T(2,128)(2,1)} %stack.7), calls=%async_computation | async-start | bytes 917504 | tf_op jit(solution)/shard_map/all_to_all | solution.py:86
  20.3 8.4 %collective-permute-start.3 = (bf16[1,130,128]{2,1,0:T(8,128)(2,1)S(1)}, bf16[1,130,128]{2,1,0:T(8,128)(2,1)S(1)}, u32[]{:S(2)}, u32[]{:S(2)}) collective-permute-start(bf16[1,130,128]{2,1,0:T(8,128)(2,1)S(1)} %get-tuple-element.17), channel_id=1, source_target_pairs={{0,16},{16,32},{32,48},{48,64},{64,80},{80,96},{96,112},{1,17},{17... | collective-permute-start | bytes 99848 | tf_op jit(solution)/shard_map/ppermute | solution.py:19
  23.6 5.1 %collective-permute-start.4 = (bf16[1,130,128]{2,1,0:T(8,128)(2,1)S(1)}, bf16[1,130,128]{2,1,0:T(8,128)(2,1)S(1)}, u32[]{:S(2)}, u32[]{:S(2)}) collective-permute-start(bf16[1,130,128]{2,1,0:T(8,128)(2,1)S(1)} %get-tuple-element.18), channel_id=1, source_target_pairs={{16,0},{32,16},{48,32},{64,48},{80,64},{96,80},{112,96},{17,1},{33... | collective-permute-start | bytes 99848 | tf_op jit(solution)/shard_map/ppermute | solution.py:21
  24.9 4.7 %collective-permute-start.2 = (bf16[2,130,128]{2,1,0:T(8,128)(2,1)S(1)}, bf16[2,130,128]{2,1,0:T(8,128)(2,1)S(1)}, u32[]{:S(2)}, u32[]{:S(2)}) collective-permute-start(bf16[2,130,128]{2,1,0:T(8,128)(2,1)S(1)} %pad_maximum_fusion.6), channel_id=1, source_target_pairs={{8,0},{9,1},{10,2},{11,3},{12,4},{13,5},{14,6},{15,7},{0,8},{1,9},... | collective-permute-start | bytes 199688 | tf_op jit(solution)/shard_map/ppermute | solution.py:31
  28.6 10.6 %copy-start.2 = (bf16[128,128,128]{2,1,0:T(8,128)(2,1)S(1)}, bf16[128,128,128]{2,1,0:T(8,128)(2,1)}, u32[]{:S(2)}) copy-start(bf16[128,128,128]{2,1,0:T(8,128)(2,1)} %param.6) | copy-start | bytes 12582916
  75.4 4.5 %copy-start.3 = (bf16[128,128,128]{2,1,0:T(8,128)(2,1)S(1)}, bf16[128,128,128]{2,1,0:T(8,128)(2,1)}, u32[]{:S(2)}) copy-start(bf16[128,128,128]{2,1,0:T(8,128)(2,1)} %param.6) | copy-start | bytes 12582916
  98.8 12.1 %copy-start = (bf16[16384,128]{1,0:T(8,128)(2,1)}, bf16[16384,128]{1,0:T(8,128)(2,1)S(1)}, u32[]{:S(2)}) copy-start(bf16[16384,128]{1,0:T(8,128)(2,1)S(1)} %fusion.25) | copy-start | bytes 12582916
  98.9 6.0 %collective-permute-start.5 = (bf16[128,1,128]{2,1,0:T(2,128)(2,1)S(1)}, bf16[128,1,128]{2,1,0:T(2,128)(2,1)S(1)}, u32[]{:S(2)}, u32[]{:S(2)}) collective-permute-start(bf16[128,1,128]{2,1,0:T(2,128)(2,1)S(1)} %get-tuple-element.19), channel_id=1, source_target_pairs={{0,1},{1,2},{2,3},{3,4},{4,5},{5,6},{6,7},{7,8},{8,9},{9,10},{10,1... | collective-permute-start | bytes 98312 | tf_op jit(solution)/shard_map/ppermute | solution.py:19
  103.5 7.3 %collective-permute-start.6 = (bf16[128,1,128]{2,1,0:T(2,128)(2,1)S(1)}, bf16[128,1,128]{2,1,0:T(2,128)(2,1)S(1)}, u32[]{:S(2)}, u32[]{:S(2)}) collective-permute-start(bf16[128,1,128]{2,1,0:T(2,128)(2,1)S(1)} %get-tuple-element.20), channel_id=1, source_target_pairs={{1,0},{2,1},{3,2},{4,3},{5,4},{6,5},{7,6},{8,7},{9,8},{10,9},{11,1... | collective-permute-start | bytes 98312 | tf_op jit(solution)/shard_map/ppermute | solution.py:21
  110.9 10.0 %collective-permute-start.7 = (bf16[2,130,128]{2,1,0:T(8,128)(2,1)S(1)}, bf16[2,130,128]{2,1,0:T(8,128)(2,1)S(1)}, u32[]{:S(2)}, u32[]{:S(2)}) collective-permute-start(bf16[2,130,128]{2,1,0:T(8,128)(2,1)S(1)} %pad_maximum_fusion.7), channel_id=1, source_target_pairs={{8,0},{9,1},{10,2},{11,3},{12,4},{13,5},{14,6},{15,7},{0,8},{1,9},... | collective-permute-start | bytes 199688 | tf_op jit(solution)/shard_map/ppermute | solution.py:31
  111.0 5.9 %collective-permute-start.8 = (bf16[1,130,128]{2,1,0:T(8,128)(2,1)S(1)}, bf16[1,130,128]{2,1,0:T(8,128)(2,1)S(1)}, u32[]{:S(2)}, u32[]{:S(2)}) collective-permute-start(bf16[1,130,128]{2,1,0:T(8,128)(2,1)S(1)} %get-tuple-element.13), channel_id=1, source_target_pairs={{0,16},{16,32},{32,48},{48,64},{64,80},{80,96},{96,112},{1,17},{17... | collective-permute-start | bytes 99848 | tf_op jit(solution)/shard_map/ppermute | solution.py:19
  115.5 5.4 %collective-permute-start.9 = (bf16[1,130,128]{2,1,0:T(8,128)(2,1)S(1)}, bf16[1,130,128]{2,1,0:T(8,128)(2,1)S(1)}, u32[]{:S(2)}, u32[]{:S(2)}) collective-permute-start(bf16[1,130,128]{2,1,0:T(8,128)(2,1)S(1)} %get-tuple-element.14), channel_id=1, source_target_pairs={{16,0},{32,16},{48,32},{64,48},{80,64},{96,80},{112,96},{17,1},{33... | collective-permute-start | bytes 99848 | tf_op jit(solution)/shard_map/ppermute | solution.py:21
  116.9 13.7 %copy-start.1 = (bf16[16384,128]{1,0:T(8,128)(2,1)S(1)}, bf16[16384,128]{1,0:T(8,128)(2,1)}, u32[]{:S(2)}) copy-start(bf16[16384,128]{1,0:T(8,128)(2,1)} %copy-done) | copy-start | bytes 12582916
